TPU v7x, 128 devices: a whole 4x4x4 slice. The times are simulated.
128 devices in a mesh: section: 8 (over x, core), tp: 16 (over z, y).
Axes of the slice: x: 4, y: 4, z: 4, core: 2. Of those that a mesh axis runs over, the one named last changes fastest.
Arguments:
- layer_inputs: bfloat16 [16, 512, 4096], P('section', None, 'tp'), may hold values from -6 to 6
- weights: bfloat16 [16, 4096, 4096], P('section', 'tp'), may hold values from -0.046875 to 0.046875
- input_basis: bfloat16 [16, 4096, 64], P('section', 'tp'), may hold values from -0.09375 to 0.09375
- output_basis: bfloat16 [16, 4096, 32], P('section', 'tp'), may hold values from -0.09375 to 0.09375
- queries: bfloat16 [16, 512, 2048], P('section', 'tp'), may hold values from -0.00390625 to 0.00390625
- top_cotangent: bfloat16 [512, 4096], replicated, may hold values from -6 to 6
- sequence_example: int32 [4], replicated, may hold values from 0 to 1
Outputs:
- scores: float32 [2, 512], P(None, 'tp')
All inputs are finite; a program needn't handle non-finite values.
Results may differ from a plain program's by a relative error of at most 0.0094.
Values may be sent and summed in bfloat16 or wider, within the bound.
No kernel may reach another device: no remote copies, remote signals or barrier semaphores. Data moves between devices by JAX's collectives and lax.ppermute only.
A program may use at most 64 MiB of HBM per device.

v0:
```python
import jax
import jax.numpy as jnp
from jax import lax
from jax.sharding import PartitionSpec as P

SEQLEN = 128
SEQ_MB = 1
MB = 4
EXAMPLES = 2


def from_behind(value, axis, by):
    size = lax.axis_size(axis)
    pairs = [(i, i + by) for i in range(size) if 0 <= i + by < size]
    return lax.ppermute(value, axis, pairs)


def silu_parts(values):
    floats = values.astype(jnp.float32)
    logistic = jax.nn.sigmoid(floats)
    return ((floats * logistic).astype(jnp.bfloat16), logistic * (1.0 + floats * (1.0 - logistic)))


def contract_columns(portion, matrix):
    return lax.dot_general(
        portion, matrix, (((1,), (1,)), ((), ())), preferred_element_type=jnp.float32
    )


def outer_rows(out_feats, in_feats):
    joined = out_feats[:, :, :, None] * in_feats[:, :, None, :]
    return joined.reshape(joined.shape[0], joined.shape[1], -1)


def shards(
    layer_inputs, weights, input_basis, output_basis, queries, top_cotangent, sequence_example
):
    section_count = lax.axis_size("section")
    section_rank = lax.axis_index("section")
    tp_rank = lax.axis_index("tp")
    width_local = layer_inputs.shape[2]
    width_full = weights.shape[2]
    total_tokens = layer_inputs.shape[1]
    block_rows = SEQ_MB * SEQLEN
    activated, slopes = silu_parts(layer_inputs)
    partial_in = jnp.einsum(
        "ltd,ldr->tlr", activated, input_basis, preferred_element_type=jnp.float32
    )
    in_feats = lax.psum(partial_in.reshape(total_tokens, -1), "tp").reshape(partial_in.shape)
    example_index = jnp.arange(EXAMPLES, dtype=jnp.int32)
    is_top = section_rank == section_count - 1

    def fold_lower(portion):
        return contract_columns(portion, weights[0])

    def tick(tick_index, state):
        outgoing, grads, stored = state
        micro_index = tick_index - (section_count - 1 - section_rank)
        valid = (micro_index >= 0) & (micro_index < MB)
        micro_clip = jnp.clip(micro_index, 0, MB - 1)
        first_row = micro_clip * block_rows
        slope_block = lax.dynamic_slice_in_dim(slopes, first_row, block_rows, 1)
        received = from_behind(outgoing, "section", -1)
        top_block = lax.dynamic_slice_in_dim(top_cotangent, first_row, block_rows, 0)
        upper_full = jnp.where(is_top, top_block, received)
        upper_own = lax.dynamic_slice_in_dim(upper_full, tp_rank * width_local, width_local, 1)
        upper_branch = lax.dot_general(
            upper_full, weights[1], (((1,), (1,)), ((), ())), preferred_element_type=jnp.float32
        )
        middle_own = (upper_own.astype(jnp.float32) + slope_block[1] * upper_branch).astype(
            jnp.bfloat16
        )
        lower_branch = fold_lower(lax.all_gather(middle_own, "tp", axis=1, tiled=True))
        lower_own = (middle_own.astype(jnp.float32) + slope_block[0] * lower_branch).astype(
            jnp.bfloat16
        )
        new_outgoing = lax.all_gather(lower_own, "tp", axis=1, tiled=True)
        cotangents = jnp.stack([middle_own, upper_own], 0)
        partial_out = jnp.einsum(
            "lrd,ldk->rlk", cotangents, output_basis, preferred_element_type=jnp.float32
        )
        out_feats = lax.psum(partial_out.reshape(block_rows, -1), "tp").reshape(partial_out.shape)
        in_block = lax.dynamic_slice_in_dim(in_feats, first_row, block_rows, 0)
        block_examples = jnp.repeat(
            lax.dynamic_slice_in_dim(sequence_example, micro_clip * SEQ_MB, SEQ_MB, 0), SEQLEN
        )
        selector = (example_index[:, None] == block_examples[None, :]).astype(
            jnp.float32
        ) * valid.astype(jnp.float32)
        grads = grads + jnp.einsum(
            "er,rlk->lek",
            selector,
            outer_rows(out_feats, in_block),
            precision=lax.Precision.HIGHEST,
        )
        return (new_outgoing, grads, stored)

    outgoing_init = jnp.zeros((block_rows, width_full), jnp.bfloat16)
    grads_init = jnp.zeros((2, EXAMPLES, queries.shape[2]), jnp.float32)
    stored_init = jnp.zeros((1,), jnp.bfloat16)
    final_out, grads, stored = lax.fori_loop(
        0, MB + section_count - 1, tick, (outgoing_init, grads_init, stored_init)
    )
    layer_scores = jnp.einsum(
        "lek,lqk->eq", grads, queries.astype(jnp.float32), precision=lax.Precision.HIGHEST
    )
    return lax.psum(layer_scores, "section")


def solution(mesh):
    placed = (
        P("section", None, "tp"),
        P("section", "tp", None),
        P("section", "tp", None),
        P("section", "tp", None),
        P("section", "tp", None),
        P(),
        P(),
    )
    return jax.shard_map(
        shards, mesh=mesh, in_specs=placed, out_specs=P(None, "tp"), check_vma=False
    )
```

profile of v0, /device:TPU:1, one launch (start us, length us, event | category | flops | bytes accessed | tf_op | source)
XLA Modules:
  0.0 1662.4 jit_solution(13824720775074881913)
XLA Ops:
  9.2 87.7 %all-reduce.2.cloned.1.call-done = f32[512,2,64]{0,2,1:T(8,128)} async-done(((f32[512,2,64]{0,2,1:T(8,128)}), f32[512,2,64]{0,2,1:T(8,128)}) %all-reduce.2.cloned.1.call-update) | async-done | bytes 262160 | tf_op jit(solution)/shard_map/psum | solution.py:49
  98.0 1529.4 %while.18 = (s32[]{:T(128)}, bf16[128,4096]{1,0:T(8,128)(2,1)}, f32[2,2,2048]{2,1,0:T(2,128)S(1)}, pred[]{:T(512)}, s32[]{:T(128)}, /*index=5*/bf16[512,4096]{1,...) while((s32[]{:T(128)}, bf16[128,4096]{1,0:T(8,128)(2,1)}, ...), condition=%wide.region_3.4_spmd.clone, body=%wide.region_1.3_spmd.clone.sunk | while | flops 555048960 | bytes 25986044 | solution.py:101
  98.0 3.9 collective-permute-start
  101.9 13.7 collective-permute-done
  120.3 40.6 %all-gather.3.cloned.1.call-done = bf16[128,4096]{1,0:T(8,128)(2,1)} async-done(((bf16[128,256]{1,0:T(8,128)(2,1)}), bf16[128,4096]{1,0:T(8,128)(2,1)}) %all-gather.3.cloned.1.call-update) | async-done | bytes 1048592 | tf_op jit(solution)/shard_map/while/body/eval_jaxpr/all_gather | solution.py:73
  160.9 3.3 add_convert_fusion.5
  166.6 58.4 %psum.31 = f32[128,2,32]{0,2,1:T(8,128)S(1)} all-reduce(f32[128,2,32]{0,2,1:T(8,128)S(1)} %convolution_bitcast_fusion.5), channel_id=1, replica_groups=mesh['section'=8,'tp'=16] {'tp'}, use_global_device_ids=true, to_apply=%region_2.2 | all-reduce | flops 8192 | bytes 65536 | tf_op jit(solution)/shard_map/while/body/eval_jaxpr/psum | solution.py:82
  227.2 17.7 %collective-permute-start = (bf16[128,4096]{1,0:T(8,128)(2,1)}, bf16[128,4096]{1,0:T(8,128)(2,1)S(1)}, u32[]{:S(2)}, u32[]{:S(2)}) collective-permute-start(bf16[128,4096]{1,0:T(8,128)(2,1)} %get-tuple-element.465), channel_id=1, source_target_pairs={{16,0},{32,16},{48,32},{64,48},{80,64},{96,80},{112,96},{17,1},{33... | collective-permute-start | bytes 3145736 | tf_op jit(solution)/shard_map/while/body/eval_jaxpr/ppermute | solution.py:15
  244.9 13.7 collective-permute-done
  260.2 3.1 add_convert_fusion.4
  263.3 37.6 %all-gather.3.cloned.1.call-done = bf16[128,4096]{1,0:T(8,128)(2,1)} async-done(((bf16[128,256]{1,0:T(8,128)(2,1)}), bf16[128,4096]{1,0:T(8,128)(2,1)}) %all-gather.3.cloned.1.call-update) | async-done | bytes 1048592 | tf_op jit(solution)/shard_map/while/body/eval_jaxpr/all_gather | solution.py:73
  300.9 3.3 add_convert_fusion.5
  306.6 58.4 %psum.31 = f32[128,2,32]{0,2,1:T(8,128)S(1)} all-reduce(f32[128,2,32]{0,2,1:T(8,128)S(1)} %convolution_bitcast_fusion.5), channel_id=1, replica_groups=mesh['section'=8,'tp'=16] {'tp'}, use_global_device_ids=true, to_apply=%region_2.2 | all-reduce | flops 8192 | bytes 65536 | tf_op jit(solution)/shard_map/while/body/eval_jaxpr/psum | solution.py:82
  367.3 17.7 %collective-permute-start = (bf16[128,4096]{1,0:T(8,128)(2,1)}, bf16[128,4096]{1,0:T(8,128)(2,1)S(1)}, u32[]{:S(2)}, u32[]{:S(2)}) collective-permute-start(bf16[128,4096]{1,0:T(8,128)(2,1)} %get-tuple-element.465), channel_id=1, source_target_pairs={{16,0},{32,16},{48,32},{64,48},{80,64},{96,80},{112,96},{17,1},{33... | collective-permute-start | bytes 3145736 | tf_op jit(solution)/shard_map/while/body/eval_jaxpr/ppermute | solution.py:15
  385.0 13.7 collective-permute-done
  400.2 3.1 add_convert_fusion.4
  403.3 37.6 %all-gather.3.cloned.1.call-done = bf16[128,4096]{1,0:T(8,128)(2,1)} async-done(((bf16[128,256]{1,0:T(8,128)(2,1)}), bf16[128,4096]{1,0:T(8,128)(2,1)}) %all-gather.3.cloned.1.call-update) | async-done | bytes 1048592 | tf_op jit(solution)/shard_map/while/body/eval_jaxpr/all_gather | solution.py:73
  441.0 3.3 add_convert_fusion.5
  446.6 58.4 %psum.31 = f32[128,2,32]{0,2,1:T(8,128)S(1)} all-reduce(f32[128,2,32]{0,2,1:T(8,128)S(1)} %convolution_bitcast_fusion.5), channel_id=1, replica_groups=mesh['section'=8,'tp'=16] {'tp'}, use_global_device_ids=true, to_apply=%region_2.2 | all-reduce | flops 8192 | bytes 65536 | tf_op jit(solution)/shard_map/while/body/eval_jaxpr/psum | solution.py:82
  507.3 17.7 %collective-permute-start = (bf16[128,4096]{1,0:T(8,128)(2,1)}, bf16[128,4096]{1,0:T(8,128)(2,1)S(1)}, u32[]{:S(2)}, u32[]{:S(2)}) collective-permute-start(bf16[128,4096]{1,0:T(8,128)(2,1)} %get-tuple-element.465), channel_id=1, source_target_pairs={{16,0},{32,16},{48,32},{64,48},{80,64},{96,80},{112,96},{17,1},{33... | collective-permute-start | bytes 3145736 | tf_op jit(solution)/shard_map/while/body/eval_jaxpr/ppermute | solution.py:15
  525.0 13.7 collective-permute-done
  540.2 3.1 add_convert_fusion.4
  543.4 37.6 %all-gather.3.cloned.1.call-done = bf16[128,4096]{1,0:T(8,128)(2,1)} async-done(((bf16[128,256]{1,0:T(8,128)(2,1)}), bf16[128,4096]{1,0:T(8,128)(2,1)}) %all-gather.3.cloned.1.call-update) | async-done | bytes 1048592 | tf_op jit(solution)/shard_map/while/body/eval_jaxpr/all_gather | solution.py:73
  581.0 3.3 add_convert_fusion.5
  586.7 58.4 %psum.31 = f32[128,2,32]{0,2,1:T(8,128)S(1)} all-reduce(f32[128,2,32]{0,2,1:T(8,128)S(1)} %convolution_bitcast_fusion.5), channel_id=1, replica_groups=mesh['section'=8,'tp'=16] {'tp'}, use_global_device_ids=true, to_apply=%region_2.2 | all-reduce | flops 8192 | bytes 65536 | tf_op jit(solution)/shard_map/while/body/eval_jaxpr/psum | solution.py:82
  647.3 17.7 %collective-permute-start = (bf16[128,4096]{1,0:T(8,128)(2,1)}, bf16[128,4096]{1,0:T(8,128)(2,1)S(1)}, u32[]{:S(2)}, u32[]{:S(2)}) collective-permute-start(bf16[128,4096]{1,0:T(8,128)(2,1)} %get-tuple-element.465), channel_id=1, source_target_pairs={{16,0},{32,16},{48,32},{64,48},{80,64},{96,80},{112,96},{17,1},{33... | collective-permute-start | bytes 3145736 | tf_op jit(solution)/shard_map/while/body/eval_jaxpr/ppermute | solution.py:15
  665.0 13.7 collective-permute-done
  683.4 37.6 %all-gather.3.cloned.1.call-done = bf16[128,4096]{1,0:T(8,128)(2,1)} async-done(((bf16[128,256]{1,0:T(8,128)(2,1)}), bf16[128,4096]{1,0:T(8,128)(2,1)}) %all-gather.3.cloned.1.call-update) | async-done | bytes 1048592 | tf_op jit(solution)/shard_map/while/body/eval_jaxpr/all_gather | solution.py:73
  721.0 3.3 add_convert_fusion.5
  726.7 58.4 %psum.31 = f32[128,2,32]{0,2,1:T(8,128)S(1)} all-reduce(f32[128,2,32]{0,2,1:T(8,128)S(1)} %convolution_bitcast_fusion.5), channel_id=1, replica_groups=mesh['section'=8,'tp'=16] {'tp'}, use_global_device_ids=true, to_apply=%region_2.2 | all-reduce | flops 8192 | bytes 65536 | tf_op jit(solution)/shard_map/while/body/eval_jaxpr/psum | solution.py:82
  787.3 17.7 %collective-permute-start = (bf16[128,4096]{1,0:T(8,128)(2,1)}, bf16[128,4096]{1,0:T(8,128)(2,1)S(1)}, u32[]{:S(2)}, u32[]{:S(2)}) collective-permute-start(bf16[128,4096]{1,0:T(8,128)(2,1)} %get-tuple-element.465), channel_id=1, source_target_pairs={{16,0},{32,16},{48,32},{64,48},{80,64},{96,80},{112,96},{17,1},{33... | collective-permute-start | bytes 3145736 | tf_op jit(solution)/shard_map/while/body/eval_jaxpr/ppermute | solution.py:15
  805.0 13.7 collective-permute-done
  823.4 37.6 %all-gather.3.cloned.1.call-done = bf16[128,4096]{1,0:T(8,128)(2,1)} async-done(((bf16[128,256]{1,0:T(8,128)(2,1)}), bf16[128,4096]{1,0:T(8,128)(2,1)}) %all-gather.3.cloned.1.call-update) | async-done | bytes 1048592 | tf_op jit(solution)/shard_map/while/body/eval_jaxpr/all_gather | solution.py:73
  861.1 3.3 add_convert_fusion.5
  866.7 58.4 %psum.31 = f32[128,2,32]{0,2,1:T(8,128)S(1)} all-reduce(f32[128,2,32]{0,2,1:T(8,128)S(1)} %convolution_bitcast_fusion.5), channel_id=1, replica_groups=mesh['section'=8,'tp'=16] {'tp'}, use_global_device_ids=true, to_apply=%region_2.2 | all-reduce | flops 8192 | bytes 65536 | tf_op jit(solution)/shard_map/while/body/eval_jaxpr/psum | solution.py:82
  927.4 17.7 %collective-permute-start = (bf16[128,4096]{1,0:T(8,128)(2,1)}, bf16[128,4096]{1,0:T(8,128)(2,1)S(1)}, u32[]{:S(2)}, u32[]{:S(2)}) collective-permute-start(bf16[128,4096]{1,0:T(8,128)(2,1)} %get-tuple-element.465), channel_id=1, source_target_pairs={{16,0},{32,16},{48,32},{64,48},{80,64},{96,80},{112,96},{17,1},{33... | collective-permute-start | bytes 3145736 | tf_op jit(solution)/shard_map/while/body/eval_jaxpr/ppermute | solution.py:15
  945.1 13.7 collective-permute-done
  960.3 3.1 add_convert_fusion.4
  963.4 37.6 %all-gather.3.cloned.1.call-done = bf16[128,4096]{1,0:T(8,128)(2,1)} async-done(((bf16[128,256]{1,0:T(8,128)(2,1)}), bf16[128,4096]{1,0:T(8,128)(2,1)}) %all-gather.3.cloned.1.call-update) | async-done | bytes 1048592 | tf_op jit(solution)/shard_map/while/body/eval_jaxpr/all_gather | solution.py:73
  1001.1 3.3 add_convert_fusion.5
  1006.7 58.4 %psum.31 = f32[128,2,32]{0,2,1:T(8,128)S(1)} all-reduce(f32[128,2,32]{0,2,1:T(8,128)S(1)} %convolution_bitcast_fusion.5), channel_id=1, replica_groups=mesh['section'=8,'tp'=16] {'tp'}, use_global_device_ids=true, to_apply=%region_2.2 | all-reduce | flops 8192 | bytes 65536 | tf_op jit(solution)/shard_map/while/body/eval_jaxpr/psum | solution.py:82
  1067.4 17.7 %collective-permute-start = (bf16[128,4096]{1,0:T(8,128)(2,1)}, bf16[128,4096]{1,0:T(8,128)(2,1)S(1)}, u32[]{:S(2)}, u32[]{:S(2)}) collective-permute-start(bf16[128,4096]{1,0:T(8,128)(2,1)} %get-tuple-element.465), channel_id=1, source_target_pairs={{16,0},{32,16},{48,32},{64,48},{80,64},{96,80},{112,96},{17,1},{33... | collective-permute-start | bytes 3145736 | tf_op jit(solution)/shard_map/while/body/eval_jaxpr/ppermute | solution.py:15
  1085.1 13.7 collective-permute-done
  1100.3 3.1 add_convert_fusion.4
  1103.5 37.6 %all-gather.3.cloned.1.call-done = bf16[128,4096]{1,0:T(8,128)(2,1)} async-done(((bf16[128,256]{1,0:T(8,128)(2,1)}), bf16[128,4096]{1,0:T(8,128)(2,1)}) %all-gather.3.cloned.1.call-update) | async-done | bytes 1048592 | tf_op jit(solution)/shard_map/while/body/eval_jaxpr/all_gather | solution.py:73
  1141.1 3.3 add_convert_fusion.5
  1146.8 58.4 %psum.31 = f32[128,2,32]{0,2,1:T(8,128)S(1)} all-reduce(f32[128,2,32]{0,2,1:T(8,128)S(1)} %convolution_bitcast_fusion.5), channel_id=1, replica_groups=mesh['section'=8,'tp'=16] {'tp'}, use_global_device_ids=true, to_apply=%region_2.2 | all-reduce | flops 8192 | bytes 65536 | tf_op jit(solution)/shard_map/while/body/eval_jaxpr/psum | solution.py:82
  1207.4 17.7 %collective-permute-start = (bf16[128,4096]{1,0:T(8,128)(2,1)}, bf16[128,4096]{1,0:T(8,128)(2,1)S(1)}, u32[]{:S(2)}, u32[]{:S(2)}) collective-permute-start(bf16[128,4096]{1,0:T(8,128)(2,1)} %get-tuple-element.465), channel_id=1, source_target_pairs={{16,0},{32,16},{48,32},{64,48},{80,64},{96,80},{112,96},{17,1},{33... | collective-permute-start | bytes 3145736 | tf_op jit(solution)/shard_map/while/body/eval_jaxpr/ppermute | solution.py:15
  1225.1 13.7 collective-permute-done
  1240.3 3.1 add_convert_fusion.4
  1243.5 37.6 %all-gather.3.cloned.1.call-done = bf16[128,4096]{1,0:T(8,128)(2,1)} async-done(((bf16[128,256]{1,0:T(8,128)(2,1)}), bf16[128,4096]{1,0:T(8,128)(2,1)}) %all-gather.3.cloned.1.call-update) | async-done | bytes 1048592 | tf_op jit(solution)/shard_map/while/body/eval_jaxpr/all_gather | solution.py:73
  1281.1 3.3 add_convert_fusion.5
  1286.8 58.4 %psum.31 = f32[128,2,32]{0,2,1:T(8,128)S(1)} all-reduce(f32[128,2,32]{0,2,1:T(8,128)S(1)} %convolution_bitcast_fusion.5), channel_id=1, replica_groups=mesh['section'=8,'tp'=16] {'tp'}, use_global_device_ids=true, to_apply=%region_2.2 | all-reduce | flops 8192 | bytes 65536 | tf_op jit(solution)/shard_map/while/body/eval_jaxpr/psum | solution.py:82
  1347.4 17.7 %collective-permute-start = (bf16[128,4096]{1,0:T(8,128)(2,1)}, bf16[128,4096]{1,0:T(8,128)(2,1)S(1)}, u32[]{:S(2)}, u32[]{:S(2)}) collective-permute-start(bf16[128,4096]{1,0:T(8,128)(2,1)} %get-tuple-element.465), channel_id=1, source_target_pairs={{16,0},{32,16},{48,32},{64,48},{80,64},{96,80},{112,96},{17,1},{33... | collective-permute-start | bytes 3145736 | tf_op jit(solution)/shard_map/while/body/eval_jaxpr/ppermute | solution.py:15
  1365.1 13.7 collective-permute-done
  1383.5 37.6 %all-gather.3.cloned.1.call-done = bf16[128,4096]{1,0:T(8,128)(2,1)} async-done(((bf16[128,256]{1,0:T(8,128)(2,1)}), bf16[128,4096]{1,0:T(8,128)(2,1)}) %all-gather.3.cloned.1.call-update) | async-done | bytes 1048592 | tf_op jit(solution)/shard_map/while/body/eval_jaxpr/all_gather | solution.py:73
  1421.2 3.3 add_convert_fusion.5
  1426.8 58.4 %psum.31 = f32[128,2,32]{0,2,1:T(8,128)S(1)} all-reduce(f32[128,2,32]{0,2,1:T(8,128)S(1)} %convolution_bitcast_fusion.5), channel_id=1, replica_groups=mesh['section'=8,'tp'=16] {'tp'}, use_global_device_ids=true, to_apply=%region_2.2 | all-reduce | flops 8192 | bytes 65536 | tf_op jit(solution)/shard_map/while/body/eval_jaxpr/psum | solution.py:82
  1487.5 17.7 %collective-permute-start = (bf16[128,4096]{1,0:T(8,128)(2,1)}, bf16[128,4096]{1,0:T(8,128)(2,1)S(1)}, u32[]{:S(2)}, u32[]{:S(2)}) collective-permute-start(bf16[128,4096]{1,0:T(8,128)(2,1)} %get-tuple-element.465), channel_id=1, source_target_pairs={{16,0},{32,16},{48,32},{64,48},{80,64},{96,80},{112,96},{17,1},{33... | collective-permute-start | bytes 3145736 | tf_op jit(solution)/shard_map/while/body/eval_jaxpr/ppermute | solution.py:15
  1505.2 13.7 collective-permute-done
  1523.5 37.6 %all-gather.3.cloned.1.call-done = bf16[128,4096]{1,0:T(8,128)(2,1)} async-done(((bf16[128,256]{1,0:T(8,128)(2,1)}), bf16[128,4096]{1,0:T(8,128)(2,1)}) %all-gather.3.cloned.1.call-update) | async-done | bytes 1048592 | tf_op jit(solution)/shard_map/while/body/eval_jaxpr/all_gather | solution.py:73
  1561.2 3.3 add_convert_fusion.5
  1566.8 58.4 %psum.31 = f32[128,2,32]{0,2,1:T(8,128)S(1)} all-reduce(f32[128,2,32]{0,2,1:T(8,128)S(1)} %convolution_bitcast_fusion.5), channel_id=1, replica_groups=mesh['section'=8,'tp'=16] {'tp'}, use_global_device_ids=true, to_apply=%region_2.2 | all-reduce | flops 8192 | bytes 65536 | tf_op jit(solution)/shard_map/while/body/eval_jaxpr/psum | solution.py:82
  1627.8 28.1 %psum.28 = f32[2,32]{1,0:T(2,128)} all-reduce(f32[2,32]{1,0:T(2,128)S(1)} %convolution_bitcast_fusion.3), channel_id=1, replica_groups=mesh['section'=8,'tp'=16] {'section'}, use_global_device_ids=true, to_apply=%region_4.5 | all-reduce | flops 64 | bytes 512 | tf_op jit(solution)/shard_map/psum | solution.py:107
  (185 shorter events, 85.7 us)
Async XLA Ops:
  6.5 1620.9 %copy-start = (bf16[2,32,2048]{2,1,0:T(8,128)(2,1)S(1)}, bf16[2,32,2048]{2,1,0:T(8,128)(2,1)}, u32[]{:S(2)}) copy-start(bf16[2,32,2048]{2,1,0:T(8,128)(2,1)} %param.13) | copy-start | bytes 786436
  6.5 2.3 copy-start.2
  6.5 90.4 %all-reduce.2.cloned.1.call-start = ((), (), s32[]{:S(2)}) async-start(), calls=%async_computation | async-start | bytes 524288 | tf_op jit(solution)/shard_map/psum | solution.py:49
  8.8 89.2 %copy-start.3 = (bf16[2,256,32]{1,2,0:T(8,128)(2,1)S(1)}, bf16[2,256,32]{1,2,0:T(8,128)(2,1)}, u32[]{:S(2)}) copy-start(bf16[2,256,32]{1,2,0:T(8,128)(2,1)} %param.12) | copy-start | bytes 98308
  8.8 89.2 %copy-start.4 = (s32[4]{0:T(128)S(1)}, s32[4]{0:T(128)}, u32[]{:S(2)}) copy-start(s32[4]{0:T(128)} %param.15) | copy-start | bytes 52
  98.0 62.9 %all-gather.3.cloned.1.call-start = ((), (), s32[]{:S(2)}) async-start(), calls=%async_computation.1 | async-start | bytes 1114112 | tf_op jit(solution)/shard_map/while/body/eval_jaxpr/all_gather | solution.py:73
  98.0 17.6 %collective-permute-start = (bf16[128,4096]{1,0:T(8,128)(2,1)}, bf16[128,4096]{1,0:T(8,128)(2,1)S(1)}, u32[]{:S(2)}, u32[]{:S(2)}) collective-permute-start(bf16[128,4096]{1,0:T(8,128)(2,1)} %get-tuple-element.465), channel_id=1, source_target_pairs={{16,0},{32,16},{48,32},{64,48},{80,64},{96,80},{112,96},{17,1},{33... | collective-permute-start | bytes 3145736 | tf_op jit(solution)/shard_map/while/body/eval_jaxpr/ppermute | solution.py:15
  120.2 46.2 %copy-start.1 = (bf16[128,256]{1,0:T(8,128)(2,1)S(1)}, bf16[128,256]{1,0:T(8,128)(2,1)}, u32[]{:S(2)}) copy-start(bf16[128,256]{1,0:T(8,128)(2,1)} %add_convert_fusion.4) | copy-start | bytes 196612 | tf_op jit(solution)/shard_map/while
  120.2 106.9 %all-gather.5.cloned.1.call-start = ((), (), s32[]{:S(2)}) async-start(), calls=%async_computation.2 | async-start | bytes 1114112 | tf_op jit(solution)/shard_map/while/body/eval_jaxpr/all_gather | solution.py:77
  227.2 73.7 %all-gather.3.cloned.1.call-start = ((), (), s32[]{:S(2)}) async-start(), calls=%async_computation.1 | async-start | bytes 1114112 | tf_op jit(solution)/shard_map/while/body/eval_jaxpr/all_gather | solution.py:73
  227.2 31.4 %collective-permute-start = (bf16[128,4096]{1,0:T(8,128)(2,1)}, bf16[128,4096]{1,0:T(8,128)(2,1)S(1)}, u32[]{:S(2)}, u32[]{:S(2)}) collective-permute-start(bf16[128,4096]{1,0:T(8,128)(2,1)} %get-tuple-element.465), channel_id=1, source_target_pairs={{16,0},{32,16},{48,32},{64,48},{80,64},{96,80},{112,96},{17,1},{33... | collective-permute-start | bytes 3145736 | tf_op jit(solution)/shard_map/while/body/eval_jaxpr/ppermute | solution.py:15
  263.2 43.2 %copy-start.1 = (bf16[128,256]{1,0:T(8,128)(2,1)S(1)}, bf16[128,256]{1,0:T(8,128)(2,1)}, u32[]{:S(2)}) copy-start(bf16[128,256]{1,0:T(8,128)(2,1)} %add_convert_fusion.4) | copy-start | bytes 196612 | tf_op jit(solution)/shard_map/while
  263.3 103.9 %all-gather.5.cloned.1.call-start = ((), (), s32[]{:S(2)}) async-start(), calls=%async_computation.2 | async-start | bytes 1114112 | tf_op jit(solution)/shard_map/while/body/eval_jaxpr/all_gather | solution.py:77
  367.2 73.8 %all-gather.3.cloned.1.call-start = ((), (), s32[]{:S(2)}) async-start(), calls=%async_computation.1 | async-start | bytes 1114112 | tf_op jit(solution)/shard_map/while/body/eval_jaxpr/all_gather | solution.py:73
  367.3 31.4 %collective-permute-start = (bf16[128,4096]{1,0:T(8,128)(2,1)}, bf16[128,4096]{1,0:T(8,128)(2,1)S(1)}, u32[]{:S(2)}, u32[]{:S(2)}) collective-permute-start(bf16[128,4096]{1,0:T(8,128)(2,1)} %get-tuple-element.465), channel_id=1, source_target_pairs={{16,0},{32,16},{48,32},{64,48},{80,64},{96,80},{112,96},{17,1},{33... | collective-permute-start | bytes 3145736 | tf_op jit(solution)/shard_map/while/body/eval_jaxpr/ppermute | solution.py:15
  403.3 43.2 %copy-start.1 = (bf16[128,256]{1,0:T(8,128)(2,1)S(1)}, bf16[128,256]{1,0:T(8,128)(2,1)}, u32[]{:S(2)}) copy-start(bf16[128,256]{1,0:T(8,128)(2,1)} %add_convert_fusion.4) | copy-start | bytes 196612 | tf_op jit(solution)/shard_map/while
  403.3 103.9 %all-gather.5.cloned.1.call-start = ((), (), s32[]{:S(2)}) async-start(), calls=%async_computation.2 | async-start | bytes 1114112 | tf_op jit(solution)/shard_map/while/body/eval_jaxpr/all_gather | solution.py:77
  507.2 73.8 %all-gather.3.cloned.1.call-start = ((), (), s32[]{:S(2)}) async-start(), calls=%async_computation.1 | async-start | bytes 1114112 | tf_op jit(solution)/shard_map/while/body/eval_jaxpr/all_gather | solution.py:73
  507.3 31.4 %collective-permute-start = (bf16[128,4096]{1,0:T(8,128)(2,1)}, bf16[128,4096]{1,0:T(8,128)(2,1)S(1)}, u32[]{:S(2)}, u32[]{:S(2)}) collective-permute-start(bf16[128,4096]{1,0:T(8,128)(2,1)} %get-tuple-element.465), channel_id=1, source_target_pairs={{16,0},{32,16},{48,32},{64,48},{80,64},{96,80},{112,96},{17,1},{33... | collective-permute-start | bytes 3145736 | tf_op jit(solution)/shard_map/while/body/eval_jaxpr/ppermute | solution.py:15
  543.3 43.2 %copy-start.1 = (bf16[128,256]{1,0:T(8,128)(2,1)S(1)}, bf16[128,256]{1,0:T(8,128)(2,1)}, u32[]{:S(2)}) copy-start(bf16[128,256]{1,0:T(8,128)(2,1)} %add_convert_fusion.4) | copy-start | bytes 196612 | tf_op jit(solution)/shard_map/while
  543.3 103.9 %all-gather.5.cloned.1.call-start = ((), (), s32[]{:S(2)}) async-start(), calls=%async_computation.2 | async-start | bytes 1114112 | tf_op jit(solution)/shard_map/while/body/eval_jaxpr/all_gather | solution.py:77
  647.3 73.8 %all-gather.3.cloned.1.call-start = ((), (), s32[]{:S(2)}) async-start(), calls=%async_computation.1 | async-start | bytes 1114112 | tf_op jit(solution)/shard_map/while/body/eval_jaxpr/all_gather | solution.py:73
  647.3 31.4 %collective-permute-start = (bf16[128,4096]{1,0:T(8,128)(2,1)}, bf16[128,4096]{1,0:T(8,128)(2,1)S(1)}, u32[]{:S(2)}, u32[]{:S(2)}) collective-permute-start(bf16[128,4096]{1,0:T(8,128)(2,1)} %get-tuple-element.465), channel_id=1, source_target_pairs={{16,0},{32,16},{48,32},{64,48},{80,64},{96,80},{112,96},{17,1},{33... | collective-permute-start | bytes 3145736 | tf_op jit(solution)/shard_map/while/body/eval_jaxpr/ppermute | solution.py:15
  683.3 43.2 %copy-start.1 = (bf16[128,256]{1,0:T(8,128)(2,1)S(1)}, bf16[128,256]{1,0:T(8,128)(2,1)}, u32[]{:S(2)}) copy-start(bf16[128,256]{1,0:T(8,128)(2,1)} %add_convert_fusion.4) | copy-start | bytes 196612 | tf_op jit(solution)/shard_map/while
  683.3 103.9 %all-gather.5.cloned.1.call-start = ((), (), s32[]{:S(2)}) async-start(), calls=%async_computation.2 | async-start | bytes 1114112 | tf_op jit(solution)/shard_map/while/body/eval_jaxpr/all_gather | solution.py:77
  787.3 73.8 %all-gather.3.cloned.1.call-start = ((), (), s32[]{:S(2)}) async-start(), calls=%async_computation.1 | async-start | bytes 1114112 | tf_op jit(solution)/shard_map/while/body/eval_jaxpr/all_gather | solution.py:73
  787.3 31.4 %collective-permute-start = (bf16[128,4096]{1,0:T(8,128)(2,1)}, bf16[128,4096]{1,0:T(8,128)(2,1)S(1)}, u32[]{:S(2)}, u32[]{:S(2)}) collective-permute-start(bf16[128,4096]{1,0:T(8,128)(2,1)} %get-tuple-element.465), channel_id=1, source_target_pairs={{16,0},{32,16},{48,32},{64,48},{80,64},{96,80},{112,96},{17,1},{33... | collective-permute-start | bytes 3145736 | tf_op jit(solution)/shard_map/while/body/eval_jaxpr/ppermute | solution.py:15
  823.3 43.2 %copy-start.1 = (bf16[128,256]{1,0:T(8,128)(2,1)S(1)}, bf16[128,256]{1,0:T(8,128)(2,1)}, u32[]{:S(2)}) copy-start(bf16[128,256]{1,0:T(8,128)(2,1)} %add_convert_fusion.4) | copy-start | bytes 196612 | tf_op jit(solution)/shard_map/while
  823.4 103.9 %all-gather.5.cloned.1.call-start = ((), (), s32[]{:S(2)}) async-start(), calls=%async_computation.2 | async-start | bytes 1114112 | tf_op jit(solution)/shard_map/while/body/eval_jaxpr/all_gather | solution.py:77
  927.3 73.8 %all-gather.3.cloned.1.call-start = ((), (), s32[]{:S(2)}) async-start(), calls=%async_computation.1 | async-start | bytes 1114112 | tf_op jit(solution)/shard_map/while/body/eval_jaxpr/all_gather | solution.py:73
  927.4 31.4 %collective-permute-start = (bf16[128,4096]{1,0:T(8,128)(2,1)}, bf16[128,4096]{1,0:T(8,128)(2,1)S(1)}, u32[]{:S(2)}, u32[]{:S(2)}) collective-permute-start(bf16[128,4096]{1,0:T(8,128)(2,1)} %get-tuple-element.465), channel_id=1, source_target_pairs={{16,0},{32,16},{48,32},{64,48},{80,64},{96,80},{112,96},{17,1},{33... | collective-permute-start | bytes 3145736 | tf_op jit(solution)/shard_map/while/body/eval_jaxpr/ppermute | solution.py:15
  963.4 43.2 %copy-start.1 = (bf16[128,256]{1,0:T(8,128)(2,1)S(1)}, bf16[128,256]{1,0:T(8,128)(2,1)}, u32[]{:S(2)}) copy-start(bf16[128,256]{1,0:T(8,128)(2,1)} %add_convert_fusion.4) | copy-start | bytes 196612 | tf_op jit(solution)/shard_map/while
  963.4 103.9 %all-gather.5.cloned.1.call-start = ((), (), s32[]{:S(2)}) async-start(), calls=%async_computation.2 | async-start | bytes 1114112 | tf_op jit(solution)/shard_map/while/body/eval_jaxpr/all_gather | solution.py:77
  1067.3 73.8 %all-gather.3.cloned.1.call-start = ((), (), s32[]{:S(2)}) async-start(), calls=%async_computation.1 | async-start | bytes 1114112 | tf_op jit(solution)/shard_map/while/body/eval_jaxpr/all_gather | solution.py:73
  1067.4 31.4 %collective-permute-start = (bf16[128,4096]{1,0:T(8,128)(2,1)}, bf16[128,4096]{1,0:T(8,128)(2,1)S(1)}, u32[]{:S(2)}, u32[]{:S(2)}) collective-permute-start(bf16[128,4096]{1,0:T(8,128)(2,1)} %get-tuple-element.465), channel_id=1, source_target_pairs={{16,0},{32,16},{48,32},{64,48},{80,64},{96,80},{112,96},{17,1},{33... | collective-permute-start | bytes 3145736 | tf_op jit(solution)/shard_map/while/body/eval_jaxpr/ppermute | solution.py:15
  1103.4 43.2 %copy-start.1 = (bf16[128,256]{1,0:T(8,128)(2,1)S(1)}, bf16[128,256]{1,0:T(8,128)(2,1)}, u32[]{:S(2)}) copy-start(bf16[128,256]{1,0:T(8,128)(2,1)} %add_convert_fusion.4) | copy-start | bytes 196612 | tf_op jit(solution)/shard_map/while
  1103.4 103.9 %all-gather.5.cloned.1.call-start = ((), (), s32[]{:S(2)}) async-start(), calls=%async_computation.2 | async-start | bytes 1114112 | tf_op jit(solution)/shard_map/while/body/eval_jaxpr/all_gather | solution.py:77
  1207.4 73.8 %all-gather.3.cloned.1.call-start = ((), (), s32[]{:S(2)}) async-start(), calls=%async_computation.1 | async-start | bytes 1114112 | tf_op jit(solution)/shard_map/while/body/eval_jaxpr/all_gather | solution.py:73
  1207.4 31.4 %collective-permute-start = (bf16[128,4096]{1,0:T(8,128)(2,1)}, bf16[128,4096]{1,0:T(8,128)(2,1)S(1)}, u32[]{:S(2)}, u32[]{:S(2)}) collective-permute-start(bf16[128,4096]{1,0:T(8,128)(2,1)} %get-tuple-element.465), channel_id=1, source_target_pairs={{16,0},{32,16},{48,32},{64,48},{80,64},{96,80},{112,96},{17,1},{33... | collective-permute-start | bytes 3145736 | tf_op jit(solution)/shard_map/while/body/eval_jaxpr/ppermute | solution.py:15
  1243.4 43.2 %copy-start.1 = (bf16[128,256]{1,0:T(8,128)(2,1)S(1)}, bf16[128,256]{1,0:T(8,128)(2,1)}, u32[]{:S(2)}) copy-start(bf16[128,256]{1,0:T(8,128)(2,1)} %add_convert_fusion.4) | copy-start | bytes 196612 | tf_op jit(solution)/shard_map/while
  1243.4 103.9 %all-gather.5.cloned.1.call-start = ((), (), s32[]{:S(2)}) async-start(), calls=%async_computation.2 | async-start | bytes 1114112 | tf_op jit(solution)/shard_map/while/body/eval_jaxpr/all_gather | solution.py:77
  1347.4 73.8 %all-gather.3.cloned.1.call-start = ((), (), s32[]{:S(2)}) async-start(), calls=%async_computation.1 | async-start | bytes 1114112 | tf_op jit(solution)/shard_map/while/body/eval_jaxpr/all_gather | solution.py:73
  1347.4 31.4 %collective-permute-start = (bf16[128,4096]{1,0:T(8,128)(2,1)}, bf16[128,4096]{1,0:T(8,128)(2,1)S(1)}, u32[]{:S(2)}, u32[]{:S(2)}) collective-permute-start(bf16[128,4096]{1,0:T(8,128)(2,1)} %get-tuple-element.465), channel_id=1, source_target_pairs={{16,0},{32,16},{48,32},{64,48},{80,64},{96,80},{112,96},{17,1},{33... | collective-permute-start | bytes 3145736 | tf_op jit(solution)/shard_map/while/body/eval_jaxpr/ppermute | solution.py:15
  1383.4 43.2 %copy-start.1 = (bf16[128,256]{1,0:T(8,128)(2,1)S(1)}, bf16[128,256]{1,0:T(8,128)(2,1)}, u32[]{:S(2)}) copy-start(bf16[128,256]{1,0:T(8,128)(2,1)} %add_convert_fusion.4) | copy-start | bytes 196612 | tf_op jit(solution)/shard_map/while
  1383.5 103.9 %all-gather.5.cloned.1.call-start = ((), (), s32[]{:S(2)}) async-start(), calls=%async_computation.2 | async-start | bytes 1114112 | tf_op jit(solution)/shard_map/while/body/eval_jaxpr/all_gather | solution.py:77
  1487.4 73.8 %all-gather.3.cloned.1.call-start = ((), (), s32[]{:S(2)}) async-start(), calls=%async_computation.1 | async-start | bytes 1114112 | tf_op jit(solution)/shard_map/while/body/eval_jaxpr/all_gather | solution.py:73
  1487.5 31.4 %collective-permute-start = (bf16[128,4096]{1,0:T(8,128)(2,1)}, bf16[128,4096]{1,0:T(8,128)(2,1)S(1)}, u32[]{:S(2)}, u32[]{:S(2)}) collective-permute-start(bf16[128,4096]{1,0:T(8,128)(2,1)} %get-tuple-element.465), channel_id=1, source_target_pairs={{16,0},{32,16},{48,32},{64,48},{80,64},{96,80},{112,96},{17,1},{33... | collective-permute-start | bytes 3145736 | tf_op jit(solution)/shard_map/while/body/eval_jaxpr/ppermute | solution.py:15
  1523.5 43.2 %copy-start.1 = (bf16[128,256]{1,0:T(8,128)(2,1)S(1)}, bf16[128,256]{1,0:T(8,128)(2,1)}, u32[]{:S(2)}) copy-start(bf16[128,256]{1,0:T(8,128)(2,1)} %add_convert_fusion.4) | copy-start | bytes 196612 | tf_op jit(solution)/shard_map/while
  1523.5 103.9 %all-gather.5.cloned.1.call-start = ((), (), s32[]{:S(2)}) async-start(), calls=%async_computation.2 | async-start | bytes 1114112 | tf_op jit(solution)/shard_map/while/body/eval_jaxpr/all_gather | solution.py:77
Sparse Core Ops, SparseCore 0:
  10.5 86.3 all-reduce.1
  120.3 40.5 all-gather.2
  164.4 42.9 all-gather.4
  263.4 37.5 all-gather.2
  304.4 42.9 all-gather.4
  403.4 37.5 all-gather.2
  444.4 42.9 all-gather.4
  543.4 37.5 all-gather.2
  584.5 42.9 all-gather.4
  683.4 37.5 all-gather.2
  724.5 42.9 all-gather.4
  823.5 37.5 all-gather.2
  864.5 42.9 all-gather.4
  963.5 37.5 all-gather.2
  1004.5 42.9 all-gather.4
  1103.5 37.5 all-gather.2
  1144.6 42.9 all-gather.4
  1243.5 37.5 all-gather.2
  1284.6 42.9 all-gather.4
  1383.6 37.5 all-gather.2
  1424.6 42.9 all-gather.4
  1523.6 37.5 all-gather.2
  1564.6 42.9 all-gather.4
where the time goes:
time: 1660 us
  blocking collectives  671 us (40%)
  waiting for transfers between devices  657 us (40%)
  starting transfers between devices  182 us (11%)
  matrix products  95 us (6%)
  other arithmetic  26.3 us (2%)
  local copies, waits for them, and re-layouts  17.8 us (1%)
    psum x11, blocking collectives, tick(): lax.psum(partial_out.reshape(block_rows, -1), 'tp')  643 us
    all_gather x11, waiting for transfers between devices, tick(): lax.all_gather(middle_own, 'tp', axis=1, tiled=True)  417 us
    ppermute x11, starting transfers between devices, from_behind(): return lax.ppermute(value, axis, pairs)  181 us
    ppermute x11, waiting for transfers between devices, from_behind(): return lax.ppermute(value, axis, pairs)  151 us
    psum x1, waiting for transfers between devices, shards(): lax.psum(partial_in.reshape(total_tokens, -1), 'tp')  87.7 us
    dot_general x11, matrix products, contract_columns(): lax.dot_general(portion, matrix, (((1,), (1,)), ((), ())), preferred_elem...  36.4 us
    dot_general x11, matrix products, tick(): lax.dot_general(upper_full, weights[1], (((1,), (1,)), ((), ())), preferr...  33.7 us
  transfers between devices with their start and end apart: 34, of which 23 were waited for; matrix products, arithmetic and copies ran while one was open for 3% of the time, Pallas kernels for 0%

commit v1 on v0

--- a/solution.py
+++ b/solution.py
@@ -7,6 +7,11 @@
 SEQ_MB = 1
 MB = 4
 EXAMPLES = 2
+
+
+def all_by_exchange(value, axis, d):
+    stack = jnp.stack([value] * lax.axis_size(axis))
+    return jnp.concatenate(lax.all_to_all(stack, axis, 0, 0), axis=d)
 
 
 def from_behind(value, axis, by):
@@ -70,7 +75,7 @@
         middle_own = (upper_own.astype(jnp.float32) + slope_block[1] * upper_branch).astype(
             jnp.bfloat16
         )
-        lower_branch = fold_lower(lax.all_gather(middle_own, "tp", axis=1, tiled=True))
+        lower_branch = fold_lower(all_by_exchange(middle_own, "tp", 1))
         lower_own = (middle_own.astype(jnp.float32) + slope_block[0] * lower_branch).astype(
             jnp.bfloat16
         )

time: 1660 us -> 1380 us (0.83)
  waiting for transfers between devices: 657 us -> 388 us
  starting transfers between devices: 182 us -> 28.1 us
  blocking collectives: 671 us -> 810 us
    all_gather x11 -> x0, waiting for transfers between devices: 417 us -> none  [tick(): lax.all_gather(middle_own, 'tp', axis=1, tiled=True)]
    all_to_all x0 -> x11, blocking collectives: none -> 161 us  [all_by_exchange(): return jnp.concatenate(lax.all_to_all(stack, axis, 0, 0), axis=d)]
    ppermute x11, starting transfers between devices: 181 us -> 27.7 us  [from_behind(): return lax.ppermute(value, axis, pairs)]
    ppermute x11, waiting for transfers between devices: 151 us -> 299 us  [from_behind(): return lax.ppermute(value, axis, pairs)]
    psum x11, blocking collectives: 643 us -> 624 us  [tick(): lax.psum(partial_out.reshape(block_rows, -1), 'tp')]
  transfers between devices with their start and end apart: 34 -> 23, of which waited for: 23 -> 12; matrix products, arithmetic and copies ran while one was open for 3% -> 4% of each run, Pallas kernels for 0% -> 0%
where the time goes in v1:
time: 1380 us; the launch traced here: 1370 us
  blocking collectives  810 us (59%)
  waiting for transfers between devices  388 us (28%)
  matrix products  85.4 us (6%)
  starting transfers between devices  28.1 us (2%)
  other arithmetic  26.1 us (2%)
  local copies, waits for them, and re-layouts  21.2 us (2%)
    psum x11, blocking collectives, tick(): lax.psum(partial_out.reshape(block_rows, -1), 'tp')  624 us
    ppermute x11, waiting for transfers between devices, from_behind(): return lax.ppermute(value, axis, pairs)  299 us
    all_to_all x11, blocking collectives, all_by_exchange(): return jnp.concatenate(lax.all_to_all(stack, axis, 0, 0), axis=d)  161 us
    psum x1, waiting for transfers between devices, shards(): lax.psum(partial_in.reshape(total_tokens, -1), 'tp')  87.7 us
    dot_general x11, matrix products, contract_columns(): lax.dot_general(portion, matrix, (((1,), (1,)), ((), ())), preferred_elem...  33.7 us
    ppermute x11, starting transfers between devices, from_behind(): return lax.ppermute(value, axis, pairs)  27.7 us
  transfers between devices with their start and end apart: 23, of which 12 were waited for; matrix products, arithmetic and copies ran while one was open for 4% of the time, Pallas kernels for 0%

profile of v1, /device:TPU:1, one launch (start us, length us, event | category | flops | bytes accessed | tf_op | source)
XLA Modules:
  0.0 1372.8 jit_solution(4297888419931333008)
XLA Ops:
  6.5 2.2 convolution_bitcast_fusion.2
  9.2 87.7 %all-reduce.2.cloned.1.call-done = f32[512,2,64]{0,2,1:T(8,128)} async-done(((f32[512,2,64]{0,2,1:T(8,128)}), f32[512,2,64]{0,2,1:T(8,128)}) %all-reduce.2.cloned.1.call-update) | async-done | bytes 262160 | tf_op jit(solution)/shard_map/psum | solution.py:54
  98.0 1243.4 %while.18 = (s32[]{:T(128)}, bf16[128,4096]{1,0:T(8,128)(2,1)}, f32[2,2,2048]{2,1,0:T(2,128)S(1)}, pred[]{:T(512)}, s32[]{:T(128)}, /*index=5*/bf16[512,4096]{1,...) while((s32[]{:T(128)}, bf16[128,4096]{1,0:T(8,128)(2,1)}, ...), condition=%wide.region_3.4_spmd.clone, body=%wide.region_1.3_spmd.clone.sunk | while | flops 555048960 | bytes 25723832 | solution.py:106
  98.0 3.9 collective-permute-start
  101.9 13.7 %collective-permute-done = bf16[128,4096]{1,0:T(8,128)(2,1)S(1)} collective-permute-done((bf16[128,4096]{1,0:T(8,128)(2,1)}, bf16[128,4096]{1,0:T(8,128)(2,1)S(1)}, u32[]{:S(2)}, u32[]{:S(2)}) %collective-permute-start) | collective-permute-done | bytes 1048608 | tf_op jit(solution)/shard_map/while/body/eval_jaxpr/ppermute | solution.py:20
  117.1 2.4 add_convert_fusion.4
  119.9 16.3 %all_to_all.13 = bf16[16,128,256]{1,2,0:T(8,128)(2,1)S(1)} all-to-all(bf16[16,128,256]{1,2,0:T(8,128)(2,1)S(1)} %stack.53), channel_id=1, replica_groups=mesh['section'=8,'tp'=16] {'tp'}, dimensions={0} | all-to-all | bytes 2097152 | tf_op jit(solution)/shard_map/while/body/eval_jaxpr/all_to_all | solution.py:14
  136.2 3.1 add_convert_fusion.5
  141.6 56.6 %psum.31 = f32[128,2,32]{0,2,1:T(8,128)S(1)} all-reduce(f32[128,2,32]{0,2,1:T(8,128)S(1)} %convolution_bitcast_fusion.5), channel_id=1, replica_groups=mesh['section'=8,'tp'=16] {'tp'}, use_global_device_ids=true, to_apply=%region_2.2 | all-reduce | flops 8192 | bytes 65536 | tf_op jit(solution)/shard_map/while/body/eval_jaxpr/psum | solution.py:87
  200.4 6.5 collective-permute-start
  207.0 28.8 %collective-permute-done = bf16[128,4096]{1,0:T(8,128)(2,1)S(1)} collective-permute-done((bf16[128,4096]{1,0:T(8,128)(2,1)}, bf16[128,4096]{1,0:T(8,128)(2,1)S(1)}, u32[]{:S(2)}, u32[]{:S(2)}) %collective-permute-start) | collective-permute-done | bytes 1048608 | tf_op jit(solution)/shard_map/while/body/eval_jaxpr/ppermute | solution.py:20
  237.3 2.4 add_convert_fusion.4
  240.1 14.5 %all_to_all.13 = bf16[16,128,256]{1,2,0:T(8,128)(2,1)S(1)} all-to-all(bf16[16,128,256]{1,2,0:T(8,128)(2,1)S(1)} %stack.53), channel_id=1, replica_groups=mesh['section'=8,'tp'=16] {'tp'}, dimensions={0} | all-to-all | bytes 2097152 | tf_op jit(solution)/shard_map/while/body/eval_jaxpr/all_to_all | solution.py:14
  254.6 3.1 add_convert_fusion.5
  260.0 56.5 %psum.31 = f32[128,2,32]{0,2,1:T(8,128)S(1)} all-reduce(f32[128,2,32]{0,2,1:T(8,128)S(1)} %convolution_bitcast_fusion.5), channel_id=1, replica_groups=mesh['section'=8,'tp'=16] {'tp'}, use_global_device_ids=true, to_apply=%region_2.2 | all-reduce | flops 8192 | bytes 65536 | tf_op jit(solution)/shard_map/while/body/eval_jaxpr/psum | solution.py:87
  318.7 1.9 collective-permute-start
  320.6 32.6 %collective-permute-done = bf16[128,4096]{1,0:T(8,128)(2,1)S(1)} collective-permute-done((bf16[128,4096]{1,0:T(8,128)(2,1)}, bf16[128,4096]{1,0:T(8,128)(2,1)S(1)}, u32[]{:S(2)}, u32[]{:S(2)}) %collective-permute-start) | collective-permute-done | bytes 1048608 | tf_op jit(solution)/shard_map/while/body/eval_jaxpr/ppermute | solution.py:20
  354.7 2.4 add_convert_fusion.4
  357.4 14.6 %all_to_all.13 = bf16[16,128,256]{1,2,0:T(8,128)(2,1)S(1)} all-to-all(bf16[16,128,256]{1,2,0:T(8,128)(2,1)S(1)} %stack.53), channel_id=1, replica_groups=mesh['section'=8,'tp'=16] {'tp'}, dimensions={0} | all-to-all | bytes 2097152 | tf_op jit(solution)/shard_map/while/body/eval_jaxpr/all_to_all | solution.py:14
  372.0 3.1 add_convert_fusion.5
  377.4 56.6 %psum.31 = f32[128,2,32]{0,2,1:T(8,128)S(1)} all-reduce(f32[128,2,32]{0,2,1:T(8,128)S(1)} %convolution_bitcast_fusion.5), channel_id=1, replica_groups=mesh['section'=8,'tp'=16] {'tp'}, use_global_device_ids=true, to_apply=%region_2.2 | all-reduce | flops 8192 | bytes 65536 | tf_op jit(solution)/shard_map/while/body/eval_jaxpr/psum | solution.py:87
  436.2 1.9 collective-permute-start
  438.1 30.5 %collective-permute-done = bf16[128,4096]{1,0:T(8,128)(2,1)S(1)} collective-permute-done((bf16[128,4096]{1,0:T(8,128)(2,1)}, bf16[128,4096]{1,0:T(8,128)(2,1)S(1)}, u32[]{:S(2)}, u32[]{:S(2)}) %collective-permute-start) | collective-permute-done | bytes 1048608 | tf_op jit(solution)/shard_map/while/body/eval_jaxpr/ppermute | solution.py:20
  470.1 2.4 add_convert_fusion.4
  472.9 14.5 %all_to_all.13 = bf16[16,128,256]{1,2,0:T(8,128)(2,1)S(1)} all-to-all(bf16[16,128,256]{1,2,0:T(8,128)(2,1)S(1)} %stack.53), channel_id=1, replica_groups=mesh['section'=8,'tp'=16] {'tp'}, dimensions={0} | all-to-all | bytes 2097152 | tf_op jit(solution)/shard_map/while/body/eval_jaxpr/all_to_all | solution.py:14
  487.4 3.1 add_convert_fusion.5
  492.8 56.3 %psum.31 = f32[128,2,32]{0,2,1:T(8,128)S(1)} all-reduce(f32[128,2,32]{0,2,1:T(8,128)S(1)} %convolution_bitcast_fusion.5), channel_id=1, replica_groups=mesh['section'=8,'tp'=16] {'tp'}, use_global_device_ids=true, to_apply=%region_2.2 | all-reduce | flops 8192 | bytes 65536 | tf_op jit(solution)/shard_map/while/body/eval_jaxpr/psum | solution.py:87
  551.4 1.9 collective-permute-start
  553.3 28.1 %collective-permute-done = bf16[128,4096]{1,0:T(8,128)(2,1)S(1)} collective-permute-done((bf16[128,4096]{1,0:T(8,128)(2,1)}, bf16[128,4096]{1,0:T(8,128)(2,1)S(1)}, u32[]{:S(2)}, u32[]{:S(2)}) %collective-permute-start) | collective-permute-done | bytes 1048608 | tf_op jit(solution)/shard_map/while/body/eval_jaxpr/ppermute | solution.py:20
  582.9 2.4 add_convert_fusion.4
  585.7 14.5 %all_to_all.13 = bf16[16,128,256]{1,2,0:T(8,128)(2,1)S(1)} all-to-all(bf16[16,128,256]{1,2,0:T(8,128)(2,1)S(1)} %stack.53), channel_id=1, replica_groups=mesh['section'=8,'tp'=16] {'tp'}, dimensions={0} | all-to-all | bytes 2097152 | tf_op jit(solution)/shard_map/while/body/eval_jaxpr/all_to_all | solution.py:14
  600.1 3.1 add_convert_fusion.5
  605.5 56.9 %psum.31 = f32[128,2,32]{0,2,1:T(8,128)S(1)} all-reduce(f32[128,2,32]{0,2,1:T(8,128)S(1)} %convolution_bitcast_fusion.5), channel_id=1, replica_groups=mesh['section'=8,'tp'=16] {'tp'}, use_global_device_ids=true, to_apply=%region_2.2 | all-reduce | flops 8192 | bytes 65536 | tf_op jit(solution)/shard_map/while/body/eval_jaxpr/psum | solution.py:87
  666.6 27.6 %collective-permute-done = bf16[128,4096]{1,0:T(8,128)(2,1)S(1)} collective-permute-done((bf16[128,4096]{1,0:T(8,128)(2,1)}, bf16[128,4096]{1,0:T(8,128)(2,1)S(1)}, u32[]{:S(2)}, u32[]{:S(2)}) %collective-permute-start) | collective-permute-done | bytes 1048608 | tf_op jit(solution)/shard_map/while/body/eval_jaxpr/ppermute | solution.py:20
  695.7 2.4 add_convert_fusion.4
  698.4 14.5 %all_to_all.13 = bf16[16,128,256]{1,2,0:T(8,128)(2,1)S(1)} all-to-all(bf16[16,128,256]{1,2,0:T(8,128)(2,1)S(1)} %stack.53), channel_id=1, replica_groups=mesh['section'=8,'tp'=16] {'tp'}, dimensions={0} | all-to-all | bytes 2097152 | tf_op jit(solution)/shard_map/while/body/eval_jaxpr/all_to_all | solution.py:14
  712.9 3.1 add_convert_fusion.5
  718.3 56.9 %psum.31 = f32[128,2,32]{0,2,1:T(8,128)S(1)} all-reduce(f32[128,2,32]{0,2,1:T(8,128)S(1)} %convolution_bitcast_fusion.5), channel_id=1, replica_groups=mesh['section'=8,'tp'=16] {'tp'}, use_global_device_ids=true, to_apply=%region_2.2 | all-reduce | flops 8192 | bytes 65536 | tf_op jit(solution)/shard_map/while/body/eval_jaxpr/psum | solution.py:87
  779.4 27.6 %collective-permute-done = bf16[128,4096]{1,0:T(8,128)(2,1)S(1)} collective-permute-done((bf16[128,4096]{1,0:T(8,128)(2,1)}, bf16[128,4096]{1,0:T(8,128)(2,1)S(1)}, u32[]{:S(2)}, u32[]{:S(2)}) %collective-permute-start) | collective-permute-done | bytes 1048608 | tf_op jit(solution)/shard_map/while/body/eval_jaxpr/ppermute | solution.py:20
  808.4 2.4 add_convert_fusion.4
  811.2 14.5 %all_to_all.13 = bf16[16,128,256]{1,2,0:T(8,128)(2,1)S(1)} all-to-all(bf16[16,128,256]{1,2,0:T(8,128)(2,1)S(1)} %stack.53), channel_id=1, replica_groups=mesh['section'=8,'tp'=16] {'tp'}, dimensions={0} | all-to-all | bytes 2097152 | tf_op jit(solution)/shard_map/while/body/eval_jaxpr/all_to_all | solution.py:14
  825.7 3.1 add_convert_fusion.5
  831.1 56.9 %psum.31 = f32[128,2,32]{0,2,1:T(8,128)S(1)} all-reduce(f32[128,2,32]{0,2,1:T(8,128)S(1)} %convolution_bitcast_fusion.5), channel_id=1, replica_groups=mesh['section'=8,'tp'=16] {'tp'}, use_global_device_ids=true, to_apply=%region_2.2 | all-reduce | flops 8192 | bytes 65536 | tf_op jit(solution)/shard_map/while/body/eval_jaxpr/psum | solution.py:87
  892.2 27.6 %collective-permute-done = bf16[128,4096]{1,0:T(8,128)(2,1)S(1)} collective-permute-done((bf16[128,4096]{1,0:T(8,128)(2,1)}, bf16[128,4096]{1,0:T(8,128)(2,1)S(1)}, u32[]{:S(2)}, u32[]{:S(2)}) %collective-permute-start) | collective-permute-done | bytes 1048608 | tf_op jit(solution)/shard_map/while/body/eval_jaxpr/ppermute | solution.py:20
  921.3 2.4 add_convert_fusion.4
  924.0 14.5 %all_to_all.13 = bf16[16,128,256]{1,2,0:T(8,128)(2,1)S(1)} all-to-all(bf16[16,128,256]{1,2,0:T(8,128)(2,1)S(1)} %stack.53), channel_id=1, replica_groups=mesh['section'=8,'tp'=16] {'tp'}, dimensions={0} | all-to-all | bytes 2097152 | tf_op jit(solution)/shard_map/while/body/eval_jaxpr/all_to_all | solution.py:14
  938.5 3.1 add_convert_fusion.5
  943.9 56.9 %psum.31 = f32[128,2,32]{0,2,1:T(8,128)S(1)} all-reduce(f32[128,2,32]{0,2,1:T(8,128)S(1)} %convolution_bitcast_fusion.5), channel_id=1, replica_groups=mesh['section'=8,'tp'=16] {'tp'}, use_global_device_ids=true, to_apply=%region_2.2 | all-reduce | flops 8192 | bytes 65536 | tf_op jit(solution)/shard_map/while/body/eval_jaxpr/psum | solution.py:87
  1005.0 27.6 %collective-permute-done = bf16[128,4096]{1,0:T(8,128)(2,1)S(1)} collective-permute-done((bf16[128,4096]{1,0:T(8,128)(2,1)}, bf16[128,4096]{1,0:T(8,128)(2,1)S(1)}, u32[]{:S(2)}, u32[]{:S(2)}) %collective-permute-start) | collective-permute-done | bytes 1048608 | tf_op jit(solution)/shard_map/while/body/eval_jaxpr/ppermute | solution.py:20
  1034.1 2.4 add_convert_fusion.4
  1036.8 14.5 %all_to_all.13 = bf16[16,128,256]{1,2,0:T(8,128)(2,1)S(1)} all-to-all(bf16[16,128,256]{1,2,0:T(8,128)(2,1)S(1)} %stack.53), channel_id=1, replica_groups=mesh['section'=8,'tp'=16] {'tp'}, dimensions={0} | all-to-all | bytes 2097152 | tf_op jit(solution)/shard_map/while/body/eval_jaxpr/all_to_all | solution.py:14
  1051.3 3.1 add_convert_fusion.5
  1056.7 56.9 %psum.31 = f32[128,2,32]{0,2,1:T(8,128)S(1)} all-reduce(f32[128,2,32]{0,2,1:T(8,128)S(1)} %convolution_bitcast_fusion.5), channel_id=1, replica_groups=mesh['section'=8,'tp'=16] {'tp'}, use_global_device_ids=true, to_apply=%region_2.2 | all-reduce | flops 8192 | bytes 65536 | tf_op jit(solution)/shard_map/while/body/eval_jaxpr/psum | solution.py:87
  1117.8 27.6 %collective-permute-done = bf16[128,4096]{1,0:T(8,128)(2,1)S(1)} collective-permute-done((bf16[128,4096]{1,0:T(8,128)(2,1)}, bf16[128,4096]{1,0:T(8,128)(2,1)S(1)}, u32[]{:S(2)}, u32[]{:S(2)}) %collective-permute-start) | collective-permute-done | bytes 1048608 | tf_op jit(solution)/shard_map/while/body/eval_jaxpr/ppermute | solution.py:20
  1146.9 2.4 add_convert_fusion.4
  1149.6 14.5 %all_to_all.13 = bf16[16,128,256]{1,2,0:T(8,128)(2,1)S(1)} all-to-all(bf16[16,128,256]{1,2,0:T(8,128)(2,1)S(1)} %stack.53), channel_id=1, replica_groups=mesh['section'=8,'tp'=16] {'tp'}, dimensions={0} | all-to-all | bytes 2097152 | tf_op jit(solution)/shard_map/while/body/eval_jaxpr/all_to_all | solution.py:14
  1164.1 3.1 add_convert_fusion.5
  1169.5 56.9 %psum.31 = f32[128,2,32]{0,2,1:T(8,128)S(1)} all-reduce(f32[128,2,32]{0,2,1:T(8,128)S(1)} %convolution_bitcast_fusion.5), channel_id=1, replica_groups=mesh['section'=8,'tp'=16] {'tp'}, use_global_device_ids=true, to_apply=%region_2.2 | all-reduce | flops 8192 | bytes 65536 | tf_op jit(solution)/shard_map/while/body/eval_jaxpr/psum | solution.py:87
  1230.6 27.6 %collective-permute-done = bf16[128,4096]{1,0:T(8,128)(2,1)S(1)} collective-permute-done((bf16[128,4096]{1,0:T(8,128)(2,1)}, bf16[128,4096]{1,0:T(8,128)(2,1)S(1)}, u32[]{:S(2)}, u32[]{:S(2)}) %collective-permute-start) | collective-permute-done | bytes 1048608 | tf_op jit(solution)/shard_map/while/body/eval_jaxpr/ppermute | solution.py:20
  1259.7 2.4 add_convert_fusion.4
  1262.5 14.5 %all_to_all.13 = bf16[16,128,256]{1,2,0:T(8,128)(2,1)S(1)} all-to-all(bf16[16,128,256]{1,2,0:T(8,128)(2,1)S(1)} %stack.53), channel_id=1, replica_groups=mesh['section'=8,'tp'=16] {'tp'}, dimensions={0} | all-to-all | bytes 2097152 | tf_op jit(solution)/shard_map/while/body/eval_jaxpr/all_to_all | solution.py:14
  1276.9 3.1 add_convert_fusion.5
  1282.3 56.9 %psum.31 = f32[128,2,32]{0,2,1:T(8,128)S(1)} all-reduce(f32[128,2,32]{0,2,1:T(8,128)S(1)} %convolution_bitcast_fusion.5), channel_id=1, replica_groups=mesh['section'=8,'tp'=16] {'tp'}, use_global_device_ids=true, to_apply=%region_2.2 | all-reduce | flops 8192 | bytes 65536 | tf_op jit(solution)/shard_map/while/body/eval_jaxpr/psum | solution.py:87
  1341.7 24.2 %psum.28 = f32[2,32]{1,0:T(2,128)} all-reduce(f32[2,32]{1,0:T(2,128)S(1)} %convolution_bitcast_fusion.3), channel_id=1, replica_groups=mesh['section'=8,'tp'=16] {'section'}, use_global_device_ids=true, to_apply=%region_4.5 | all-reduce | flops 64 | bytes 512 | tf_op jit(solution)/shard_map/psum | solution.py:112
  (163 shorter events, 82.3 us)
Async XLA Ops:
  6.5 1334.9 %copy-start = (bf16[2,32,2048]{2,1,0:T(8,128)(2,1)S(1)}, bf16[2,32,2048]{2,1,0:T(8,128)(2,1)}, u32[]{:S(2)}) copy-start(bf16[2,32,2048]{2,1,0:T(8,128)(2,1)} %param.13) | copy-start | bytes 786436
  6.5 2.3 copy-start.1
  6.5 90.4 %all-reduce.2.cloned.1.call-start = ((), (), s32[]{:S(2)}) async-start(), calls=%async_computation.1 | async-start | bytes 524288 | tf_op jit(solution)/shard_map/psum | solution.py:54
  8.8 89.2 %copy-start.2 = (bf16[2,256,32]{1,2,0:T(8,128)(2,1)S(1)}, bf16[2,256,32]{1,2,0:T(8,128)(2,1)}, u32[]{:S(2)}) copy-start(bf16[2,256,32]{1,2,0:T(8,128)(2,1)} %param.12) | copy-start | bytes 98308
  8.8 89.2 %copy-start.3 = (s32[4]{0:T(128)S(1)}, s32[4]{0:T(128)}, u32[]{:S(2)}) copy-start(s32[4]{0:T(128)} %param.15) | copy-start | bytes 52
  98.0 102.4 %all-gather.2.cloned.1.call-start = ((), (), s32[]{:S(2)}) async-start(), calls=%async_computation.2 | async-start | bytes 1114112 | tf_op jit(solution)/shard_map/while/body/eval_jaxpr/all_gather | solution.py:82
  98.0 17.6 %collective-permute-start = (bf16[128,4096]{1,0:T(8,128)(2,1)}, bf16[128,4096]{1,0:T(8,128)(2,1)S(1)}, u32[]{:S(2)}, u32[]{:S(2)}) collective-permute-start(bf16[128,4096]{1,0:T(8,128)(2,1)} %get-tuple-element.465), channel_id=1, source_target_pairs={{16,0},{32,16},{48,32},{64,48},{80,64},{96,80},{112,96},{17,1},{33... | collective-permute-start | bytes 3145736 | tf_op jit(solution)/shard_map/while/body/eval_jaxpr/ppermute | solution.py:20
  200.4 118.2 %all-gather.2.cloned.1.call-start = ((), (), s32[]{:S(2)}) async-start(), calls=%async_computation.2 | async-start | bytes 1114112 | tf_op jit(solution)/shard_map/while/body/eval_jaxpr/all_gather | solution.py:82
  200.4 35.4 %collective-permute-start = (bf16[128,4096]{1,0:T(8,128)(2,1)}, bf16[128,4096]{1,0:T(8,128)(2,1)S(1)}, u32[]{:S(2)}, u32[]{:S(2)}) collective-permute-start(bf16[128,4096]{1,0:T(8,128)(2,1)} %get-tuple-element.465), channel_id=1, source_target_pairs={{16,0},{32,16},{48,32},{64,48},{80,64},{96,80},{112,96},{17,1},{33... | collective-permute-start | bytes 3145736 | tf_op jit(solution)/shard_map/while/body/eval_jaxpr/ppermute | solution.py:20
  318.6 117.5 %all-gather.2.cloned.1.call-start = ((), (), s32[]{:S(2)}) async-start(), calls=%async_computation.2 | async-start | bytes 1114112 | tf_op jit(solution)/shard_map/while/body/eval_jaxpr/all_gather | solution.py:82
  318.7 34.5 %collective-permute-start = (bf16[128,4096]{1,0:T(8,128)(2,1)}, bf16[128,4096]{1,0:T(8,128)(2,1)S(1)}, u32[]{:S(2)}, u32[]{:S(2)}) collective-permute-start(bf16[128,4096]{1,0:T(8,128)(2,1)} %get-tuple-element.465), channel_id=1, source_target_pairs={{16,0},{32,16},{48,32},{64,48},{80,64},{96,80},{112,96},{17,1},{33... | collective-permute-start | bytes 3145736 | tf_op jit(solution)/shard_map/while/body/eval_jaxpr/ppermute | solution.py:20
  436.1 115.2 %all-gather.2.cloned.1.call-start = ((), (), s32[]{:S(2)}) async-start(), calls=%async_computation.2 | async-start | bytes 1114112 | tf_op jit(solution)/shard_map/while/body/eval_jaxpr/all_gather | solution.py:82
  436.2 32.5 %collective-permute-start = (bf16[128,4096]{1,0:T(8,128)(2,1)}, bf16[128,4096]{1,0:T(8,128)(2,1)S(1)}, u32[]{:S(2)}, u32[]{:S(2)}) collective-permute-start(bf16[128,4096]{1,0:T(8,128)(2,1)} %get-tuple-element.465), channel_id=1, source_target_pairs={{16,0},{32,16},{48,32},{64,48},{80,64},{96,80},{112,96},{17,1},{33... | collective-permute-start | bytes 3145736 | tf_op jit(solution)/shard_map/while/body/eval_jaxpr/ppermute | solution.py:20
  551.3 113.2 %all-gather.2.cloned.1.call-start = ((), (), s32[]{:S(2)}) async-start(), calls=%async_computation.2 | async-start | bytes 1114112 | tf_op jit(solution)/shard_map/while/body/eval_jaxpr/all_gather | solution.py:82
  551.4 30.0 %collective-permute-start = (bf16[128,4096]{1,0:T(8,128)(2,1)}, bf16[128,4096]{1,0:T(8,128)(2,1)S(1)}, u32[]{:S(2)}, u32[]{:S(2)}) collective-permute-start(bf16[128,4096]{1,0:T(8,128)(2,1)} %get-tuple-element.465), channel_id=1, source_target_pairs={{16,0},{32,16},{48,32},{64,48},{80,64},{96,80},{112,96},{17,1},{33... | collective-permute-start | bytes 3145736 | tf_op jit(solution)/shard_map/while/body/eval_jaxpr/ppermute | solution.py:20
  664.6 112.8 %all-gather.2.cloned.1.call-start = ((), (), s32[]{:S(2)}) async-start(), calls=%async_computation.2 | async-start | bytes 1114112 | tf_op jit(solution)/shard_map/while/body/eval_jaxpr/all_gather | solution.py:82
  664.6 29.6 %collective-permute-start = (bf16[128,4096]{1,0:T(8,128)(2,1)}, bf16[128,4096]{1,0:T(8,128)(2,1)S(1)}, u32[]{:S(2)}, u32[]{:S(2)}) collective-permute-start(bf16[128,4096]{1,0:T(8,128)(2,1)} %get-tuple-element.465), channel_id=1, source_target_pairs={{16,0},{32,16},{48,32},{64,48},{80,64},{96,80},{112,96},{17,1},{33... | collective-permute-start | bytes 3145736 | tf_op jit(solution)/shard_map/while/body/eval_jaxpr/ppermute | solution.py:20
  777.4 112.7 %all-gather.2.cloned.1.call-start = ((), (), s32[]{:S(2)}) async-start(), calls=%async_computation.2 | async-start | bytes 1114112 | tf_op jit(solution)/shard_map/while/body/eval_jaxpr/all_gather | solution.py:82
  777.4 29.5 %collective-permute-start = (bf16[128,4096]{1,0:T(8,128)(2,1)}, bf16[128,4096]{1,0:T(8,128)(2,1)S(1)}, u32[]{:S(2)}, u32[]{:S(2)}) collective-permute-start(bf16[128,4096]{1,0:T(8,128)(2,1)} %get-tuple-element.465), channel_id=1, source_target_pairs={{16,0},{32,16},{48,32},{64,48},{80,64},{96,80},{112,96},{17,1},{33... | collective-permute-start | bytes 3145736 | tf_op jit(solution)/shard_map/while/body/eval_jaxpr/ppermute | solution.py:20
  890.2 112.8 %all-gather.2.cloned.1.call-start = ((), (), s32[]{:S(2)}) async-start(), calls=%async_computation.2 | async-start | bytes 1114112 | tf_op jit(solution)/shard_map/while/body/eval_jaxpr/all_gather | solution.py:82
  890.2 29.6 %collective-permute-start = (bf16[128,4096]{1,0:T(8,128)(2,1)}, bf16[128,4096]{1,0:T(8,128)(2,1)S(1)}, u32[]{:S(2)}, u32[]{:S(2)}) collective-permute-start(bf16[128,4096]{1,0:T(8,128)(2,1)} %get-tuple-element.465), channel_id=1, source_target_pairs={{16,0},{32,16},{48,32},{64,48},{80,64},{96,80},{112,96},{17,1},{33... | collective-permute-start | bytes 3145736 | tf_op jit(solution)/shard_map/while/body/eval_jaxpr/ppermute | solution.py:20
  1003.0 112.8 %all-gather.2.cloned.1.call-start = ((), (), s32[]{:S(2)}) async-start(), calls=%async_computation.2 | async-start | bytes 1114112 | tf_op jit(solution)/shard_map/while/body/eval_jaxpr/all_gather | solution.py:82
  1003.0 29.6 %collective-permute-start = (bf16[128,4096]{1,0:T(8,128)(2,1)}, bf16[128,4096]{1,0:T(8,128)(2,1)S(1)}, u32[]{:S(2)}, u32[]{:S(2)}) collective-permute-start(bf16[128,4096]{1,0:T(8,128)(2,1)} %get-tuple-element.465), channel_id=1, source_target_pairs={{16,0},{32,16},{48,32},{64,48},{80,64},{96,80},{112,96},{17,1},{33... | collective-permute-start | bytes 3145736 | tf_op jit(solution)/shard_map/while/body/eval_jaxpr/ppermute | solution.py:20
  1115.8 112.8 %all-gather.2.cloned.1.call-start = ((), (), s32[]{:S(2)}) async-start(), calls=%async_computation.2 | async-start | bytes 1114112 | tf_op jit(solution)/shard_map/while/body/eval_jaxpr/all_gather | solution.py:82
  1115.8 29.6 %collective-permute-start = (bf16[128,4096]{1,0:T(8,128)(2,1)}, bf16[128,4096]{1,0:T(8,128)(2,1)S(1)}, u32[]{:S(2)}, u32[]{:S(2)}) collective-permute-start(bf16[128,4096]{1,0:T(8,128)(2,1)} %get-tuple-element.465), channel_id=1, source_target_pairs={{16,0},{32,16},{48,32},{64,48},{80,64},{96,80},{112,96},{17,1},{33... | collective-permute-start | bytes 3145736 | tf_op jit(solution)/shard_map/while/body/eval_jaxpr/ppermute | solution.py:20
  1228.6 112.8 %all-gather.2.cloned.1.call-start = ((), (), s32[]{:S(2)}) async-start(), calls=%async_computation.2 | async-start | bytes 1114112 | tf_op jit(solution)/shard_map/while/body/eval_jaxpr/all_gather | solution.py:82
  1228.7 29.6 %collective-permute-start = (bf16[128,4096]{1,0:T(8,128)(2,1)}, bf16[128,4096]{1,0:T(8,128)(2,1)S(1)}, u32[]{:S(2)}, u32[]{:S(2)}) collective-permute-start(bf16[128,4096]{1,0:T(8,128)(2,1)} %get-tuple-element.465), channel_id=1, source_target_pairs={{16,0},{32,16},{48,32},{64,48},{80,64},{96,80},{112,96},{17,1},{33... | collective-permute-start | bytes 3145736 | tf_op jit(solution)/shard_map/while/body/eval_jaxpr/ppermute | solution.py:20
Sparse Core Ops, SparseCore 0:
  10.5 86.3 all-reduce.1
  139.4 45.5 all-gather.1
  257.8 42.4 all-gather.1
  375.2 39.9 all-gather.1
  490.6 37.3 all-gather.1
  603.3 37.3 all-gather.1
  716.1 37.3 all-gather.1
  828.9 37.3 all-gather.1
  941.7 37.4 all-gather.1
  1054.5 37.3 all-gather.1
  1167.3 37.3 all-gather.1
  1280.1 37.3 all-gather.1
